TPU v7x, 256 devices: a whole 4x4x8 slice. The times are simulated.
256 devices in a mesh: cube: 16 (over z, x_hi), row: 4 (over x_lo, core), col: 4 (over y).
Axes of the slice: x: 4 (x_hi: 2, x_lo: 2; x = x_hi * 2 + x_lo), y: 4, z: 8, core: 2. Of those that a mesh axis runs over, the one named last changes fastest.
Arguments:
- diag_block: float32 [16, 512, 512], P('cube'), as said below
- panel: float32 [16, 8192, 512], P('cube', ('row', 'col')), may hold values from -2.4 to 2.4
- trailing: float32 [16, 2048, 8192], P('cube', 'col', 'row'), may hold values from -6 to 6
- parent_front: float32 [16, 512, 8192], P('cube', 'col', 'row'), may hold values from -6 to 6
- front_order: int32 [16], P('cube'), may hold values from 4096 to 8192, as said below
- dest_group: int32 [16, 4, 4, 64, 1], P(None, 'col', 'row'), may hold values from 0 to 15; in each aligned block of 64 rows (0 to 63, 64 to 127, ..., all dimensions but the last counted through in order) at most 8 rows name the same one
- parent_block: int32 [16, 4, 4, 64, 1], P(None, 'col', 'row'), may hold values from 0 to 15
Outputs:
- assembled: float32 [16, 512, 8192], P('cube', 'col', 'row')
Inputs may be any that keep to these rules, and one draw needn't show every extreme that they name: `front_order`: a multiple of 128; each group's update matrix is zero in the columns at or beyond it. `dest_group`: at most 8 of the 64 blocks of one device and group go to one group. `diag_block`: symmetric positive definite.
All inputs are finite; a program needn't handle non-finite values.
Results may differ from a plain program's by a relative error of at most 0.0003.
Values sent between devices are 32-bit elements; how exact they have to be, the bound alone decides.
A program may use at most 128 MiB of HBM per device.

v0:
```python
import jax
import jax.numpy as jnp
from jax import lax
from jax.sharding import PartitionSpec as P

BS = 128


def spread(value, axis, root):
    mine = lax.axis_index(axis) == root
    return lax.psum(jnp.where(mine, value, jnp.zeros_like(value)), axis)


def shards(diag_block, panel, trailing, parent_front, front_order, dest_group, parent_block):
    precise_mode = lax.Precision.HIGHEST
    chol_diag = jnp.linalg.cholesky(diag_block[0])
    panel_factor = lax.linalg.triangular_solve(
        chol_diag, panel[0], left_side=False, lower=True, transpose_a=True
    )
    slab_factor = spread(panel_factor, "row", 0)
    product = lax.dot_general(
        slab_factor,
        lax.all_gather(panel_factor, "col", axis=0, tiled=True),
        (((1,), (1,)), ((), ())),
        precision=precise_mode,
    )
    device_rows = trailing.shape[1]
    cols_dev = trailing.shape[2]
    column_ids = lax.axis_index("row") * cols_dev + jnp.arange(cols_dev, dtype=jnp.int32)
    update = jnp.where(
        column_ids[None, :] < front_order[0], trailing[0] - product, jnp.float32(0.0)
    )
    block_rows = device_rows // BS
    block_cols = cols_dev // BS
    blocks = (
        update.reshape(block_rows, BS, block_cols, BS)
        .transpose(0, 2, 1, 3)
        .reshape(block_rows * block_cols, BS * BS)
    )
    nblocks = block_rows * block_cols
    groups = lax.axis_size("cube")
    own_group = lax.axis_index("cube")
    dest_all = dest_group[:, 0, 0, :, 0]
    parent_all = parent_block[:, 0, 0, :, 0]
    dest_mine = lax.dynamic_index_in_dim(dest_all, own_group, 0, keepdims=False)
    parent_rows = parent_front.shape[1]
    parent_brows = parent_rows // BS
    nparent = parent_brows * block_cols
    capacity = 2 * nblocks // groups
    hit_table = (dest_mine[:, None] == jnp.arange(groups, dtype=jnp.int32)[None, :]).astype(
        jnp.int32
    )
    before = jnp.cumsum(hit_table, axis=0) - hit_table
    slot_ids = jnp.sum(before * hit_table, axis=1)
    position = dest_mine * capacity + slot_ids
    picker = (position[None, :] == jnp.arange(groups * capacity, dtype=jnp.int32)[:, None]).astype(
        jnp.float32
    )
    outgoing = jnp.dot(picker, blocks, precision=precise_mode).reshape(groups, capacity, BS * BS)
    incoming = lax.all_to_all(outgoing, "cube", split_axis=0, concat_axis=0, tiled=True)
    arriving = (dest_all == own_group).astype(jnp.int32)
    rank_ids = jnp.cumsum(arriving, axis=1) - arriving
    in_slot = (
        arriving[:, :, None]
        * (rank_ids[:, :, None] == jnp.arange(capacity, dtype=jnp.int32)[None, None, :])
    ).astype(jnp.float32)
    to_parent = (
        parent_all[:, :, None] == jnp.arange(nparent, dtype=jnp.int32)[None, None, :]
    ).astype(jnp.float32)
    weight = jnp.einsum("sbk,sbp->psk", in_slot, to_parent, precision=precise_mode)
    assembled = jnp.dot(
        weight.reshape(nparent, groups * capacity),
        incoming.reshape(groups * capacity, BS * BS),
        precision=precise_mode,
    )
    assembled = (
        assembled.reshape(parent_brows, block_cols, BS, BS)
        .transpose(0, 2, 1, 3)
        .reshape(parent_rows, cols_dev)
    )
    return (parent_front[0] + assembled)[None]


def solution(mesh):
    placed = (
        P("cube", None, None),
        P("cube", ("row", "col"), None),
        P("cube", "col", "row"),
        P("cube", "col", "row"),
        P("cube"),
        P(None, "col", "row", None, None),
        P(None, "col", "row", None, None),
    )
    return jax.shard_map(
        shards, mesh=mesh, in_specs=placed, out_specs=P("cube", "col", "row"), check_vma=False
    )
```

profile of v0, /device:TPU:1, one launch (start us, length us, event | category | flops | bytes accessed | tf_op | source)
XLA Modules:
  0.0 464.2 jit_solution(15554430962399069206)
XLA Ops:
  7.4 1.6 copy.9
  8.9 1.4 fusion.2
  10.4 11.7 %cholesky.104 = f32[128,128]{1,0:T(8,128)S(1)} custom-call(f32[128,128]{1,0:T(8,128)S(1)} %cholesky.266), custom_call_target="Cholesky" | custom-call | tf_op jit(solution)/shard_map/jit(cholesky)/cholesky | solution.py:16
  22.2 9.8 %custom-call.30 = f32[1,128,128]{1,2,0:T(8,128)S(1)} custom-call(f32[1,128,128]{2,1,0:T(8,128)S(1)} %get-tuple-element.34), custom_call_target="InvertDiagBlocksLowerTriangular" | custom-call | tf_op jit(solution)/shard_map/jit(cholesky)/cholesky | solution.py:16
  32.8 11.7 %cholesky.217 = f32[128,128]{1,0:T(8,128)S(1)} custom-call(f32[128,128]{1,0:T(8,128)S(1)} %cholesky.270), custom_call_target="Cholesky" | custom-call | tf_op jit(solution)/shard_map/jit(cholesky)/cholesky | solution.py:16
  44.5 10.0 %custom-call.31 = f32[1,128,128]{1,2,0:T(8,128)S(1)} custom-call(f32[1,128,128]{2,1,0:T(8,128)S(1)} %get-tuple-element.31), custom_call_target="InvertDiagBlocksLowerTriangular" | custom-call | tf_op jit(solution)/shard_map/jit(cholesky)/cholesky | solution.py:16
  55.2 11.7 %cholesky.238 = f32[128,128]{1,0:T(8,128)S(1)} custom-call(f32[128,128]{1,0:T(8,128)S(1)} %cholesky.275), custom_call_target="Cholesky" | custom-call | tf_op jit(solution)/shard_map/jit(cholesky)/cholesky | solution.py:16
  66.9 0.6 compare_reduce_fusion.1
  67.5 9.8 %custom-call.32 = f32[1,128,128]{1,2,0:T(8,128)S(1)} custom-call(f32[1,128,128]{2,1,0:T(8,128)S(1)} %get-tuple-element.28), custom_call_target="InvertDiagBlocksLowerTriangular" | custom-call | tf_op jit(solution)/shard_map/jit(cholesky)/cholesky | solution.py:16
  78.0 11.7 %cholesky.255 = f32[128,128]{1,0:T(8,128)S(1)} custom-call(f32[128,128]{1,0:T(8,128)S(1)} %convolution_subtract_fusion.5), custom_call_target="Cholesky" | custom-call | tf_op jit(solution)/shard_map/jit(cholesky)/cholesky | solution.py:16
  89.7 0.7 compare_reduce_fusion
  90.4 0.7 compare_reduce_fusion.2
  93.9 10.1 %while.1 = (s32[]{:T(128)}, f32[512,512]{1,0:T(8,128)S(1)}, s32[4,2]{0,1:T(2,128)S(1)}, f32[4,128,128]{2,1,0:T(8,128)}, s32[]{:T(128)}) while((s32[]{:T(128)}, f32[512,512]{1,0:T(8,128)S(1)}, s32[4,2]{0,1:T(2,128)S(1)}, f32[4,128,128]{2,1,0:T(8,128)}, s32[]{:T(128)}) %tuple.28), condition=%wide.while_cond, body=%wide.while_body.sunk | while | flops 2 | bytes 132705 | solution.py:17
  94.5 1.9 bitcast_dynamic-update-slice_fusion.2
  97.0 1.9 bitcast_dynamic-update-slice_fusion.2
  99.6 1.9 bitcast_dynamic-update-slice_fusion.2
  102.1 1.9 bitcast_dynamic-update-slice_fusion.2
  104.0 40.1 %custom-call.33 = f32[4,128,128]{1,2,0:T(8,128)S(1)} custom-call(f32[4,128,128]{2,1,0:T(8,128)} %get-tuple-element.12), custom_call_target="InvertDiagBlocksLowerTriangular" | custom-call | tf_op jit(solution)/shard_map/triangular_solve | solution.py:17
  146.7 0.8 convolution_subtract_fusion.2
  147.8 1.5 pad_maximum_fusion
  151.0 49.6 %all-reduce.3.cloned.1.call-done = f32[512,512]{1,0:T(8,128)} async-done(((f32[512,512]{1,0:T(8,128)}), f32[512,512]{1,0:T(8,128)}) %all-reduce.3.cloned.1.call-update) | async-done | bytes 1048592 | tf_op jit(solution)/shard_map/psum | solution.py:11
  200.6 5.6 %all-gather.2.cloned.1.call-done = f32[2048,512]{1,0:T(8,128)} async-done(((f32[512,512]{1,0:T(8,128)}), f32[2048,512]{1,0:T(8,128)}) %all-gather.2.cloned.1.call-update) | async-done | bytes 4194320 | tf_op jit(solution)/shard_map/all_gather | solution.py:23
  206.2 9.7 %fusion.1 = f32[64,8,16,128]{3,1,2,0:T(8,128)S(1)} fusion(f32[1,512,2048]{2,1,0:T(8,128)} %param.9, f32[512,512]{1,0:T(8,128)} %all-reduce.3.cloned.1.call-done, f32[2048,512]{1,0:T(8,128)} %all-gather.2.cloned.1.call-done, pred[2048]{0:T(1024)(128)(4,1)S(1)} %add_compare_fusion), kind=kOutput, calls=%fused_computation.5 | convolution fusion | flops 6444548096 | bytes 13633536 | tf_op jit(solution)/shard_map/dot_general | solution.py:21
  215.9 0.9 copy.27
  217.2 3.3 copy.18
  220.4 4.9 %reshape.146 = f32[64,16384,1]{1,0,2:T(8,128)} reshape(f32[4,16,128,128]{3,2,1,0:T(8,128)} %copy.18) | data formatting | bytes 8388608 | tf_op jit(solution)/shard_map/reshape | solution.py:38
  225.4 8.7 %fusion.33 = f32[16,8,16384]{2,1,0:T(8,128)} fusion(f32[64,16384,1]{1,0,2:T(8,128)} %reshape.146, s32[16,8]{1,0:T(8,128)S(1)} %multiply_add_fusion, s32[64]{0:T(128)S(1)} %multiply_add_fusion.1), kind=kOutput, calls=%fused_computation.67 | convolution fusion | flops 1610620928 | bytes 12583680 | tf_op jit(solution)/shard_map/dot_general | solution.py:59
  234.1 9.7 %all-to-all-start = ((f32[16,8,16384]{2,1,0:T(8,128)}), f32[16,8,16384]{2,1,0:T(8,128)}, u32[]{:S(2)}, u32[]{:S(2)}) async-start(f32[16,8,16384]{2,1,0:T(8,128)} %fusion.33), calls=%async_computation | async-start | bytes 16777216 | tf_op jit(solution)/shard_map/all_to_all | solution.py:60
  244.3 192.4 %all-to-all-done = f32[16,8,16384]{2,1,0:T(8,128)} async-done(((f32[16,8,16384]{2,1,0:T(8,128)}), f32[16,8,16384]{2,1,0:T(8,128)}, u32[]{:S(2)}, u32[]{:S(2)}) %all-to-all-start) | async-done | bytes 8388640 | tf_op jit(solution)/shard_map/all_to_all | solution.py:60
  436.7 9.0 %copy.19 = f32[16384,128]{1,0:T(8,128)} copy(f32[16384,128]{0,1:T(8,128)} %bitcast.26) | data formatting | bytes 16777216 | tf_op jit(solution)/shard_map/dot_general | solution.py:71
  445.7 9.4 %convolution_bitcast_fusion = f32[1,128,16,128]{3,2,1,0:T(8,128)S(1)} fusion(f32[16,128,1]{0,1,2:T(8,128)S(1)} %convolution_bitcast_fusion.1, f32[128,128,128]{2,1,0:T(8,128)} %bitcast.103), kind=kOutput, calls=%fused_computation.6 | convolution fusion | flops 402653184 | bytes 9445376 | tf_op jit(solution)/shard_map/dot_general | solution.py:71
  455.3 1.1 add.76
  (58 shorter events, 9.5 us)
Async XLA Ops:
  7.4 193.2 %all-reduce.3.cloned.1.call-start = ((), (), s32[]{:S(2)}) async-start(), calls=%async_computation.1 | async-start | bytes 2097152 | tf_op jit(solution)/shard_map/psum | solution.py:11
  10.4 133.8 %copy-start.1 = (f32[1,512,512]{2,1,0:T(8,128)S(1)}, f32[1,512,512]{2,1,0:T(8,128)}, u32[]{:S(2)}) copy-start(f32[1,512,512]{2,1,0:T(8,128)} %param.8) | copy-start | bytes 3145732
  146.3 4.3 copy-start.2
  149.4 56.8 %all-gather.2.cloned.1.call-start = ((), (), s32[]{:S(2)}) async-start(), calls=%async_computation.2 | async-start | bytes 5242880 | tf_op jit(solution)/shard_map/all_gather | solution.py:23
  234.1 10.0 %copy-start.3 = (s32[16,1,1,64,1]{3,4,2,1,0:T(1,128)S(1)}, s32[16,1,1,64,1]{3,4,2,1,0:T(1,128)}, u32[]{:S(2)}) copy-start(s32[16,1,1,64,1]{3,4,2,1,0:T(1,128)} %param.13) | copy-start | bytes 12292
  234.1 202.6 %all-to-all-start = ((f32[16,8,16384]{2,1,0:T(8,128)}), f32[16,8,16384]{2,1,0:T(8,128)}, u32[]{:S(2)}, u32[]{:S(2)}) async-start(f32[16,8,16384]{2,1,0:T(8,128)} %fusion.33), calls=%async_computation | async-start | bytes 16777216 | tf_op jit(solution)/shard_map/all_to_all | solution.py:60
  445.7 9.6 %copy-start = (f32[1,128,2048]{2,1,0:T(8,128)S(1)}, f32[1,128,2048]{2,1,0:T(8,128)}, u32[]{:S(2)}) copy-start(f32[1,128,2048]{2,1,0:T(8,128)} %param.10) | copy-start | bytes 3145732
Sparse Core Ops, SparseCore 0:
  149.5 51.0 all-reduce.2
Sparse Core Ops, SparseCore 1:
  151.8 54.4 all-gather.1
where the time goes:
time: 473 us; the launch traced here: 464 us
  waiting for transfers between devices  248 us (52%)
  other arithmetic  123 us (26%)
  matrix products  33.4 us (7%)
  local copies, waits for them, and re-layouts  30.6 us (6%)
  between operations  18.9 us (4%)
  starting transfers between devices  9.75 us (2%)
    all_to_all x1, waiting for transfers between devices, shards(): lax.all_to_all(outgoing, 'cube', split_axis=0, concat_axis=0, tiled=True)  192 us
    another operation x14, other arithmetic, shards(): chol_diag = jnp.linalg.cholesky(diag_block[0])  78.6 us
    psum x1, waiting for transfers between devices, spread(): return lax.psum(jnp.where(mine, value, jnp.zeros_like(value)), axis)  49.6 us
    another operation x4, other arithmetic, shards(): lax.linalg.triangular_solve(chol_diag, panel[0], left_side=False, lower=T...  41.8 us
    another operation x12, local copies, waits for them, and re-layouts  10.1 us
    all_to_all x1, starting transfers between devices, shards(): lax.all_to_all(outgoing, 'cube', split_axis=0, concat_axis=0, tiled=True)  9.7 us
    dot_general x1, matrix products, shards(): lax.dot_general(slab_factor, lax.all_gather(panel_factor, 'col', axis=0,...  9.67 us
  transfers between devices with their start and end apart: 3, of which 3 were waited for; matrix products, arithmetic and copies ran while one was open for 0% of the time, Pallas kernels for 0%

commit v1 on v0

--- a/solution.py
+++ b/solution.py
@@ -8,7 +8,7 @@
 
 def spread(value, axis, root):
     mine = lax.axis_index(axis) == root
-    return lax.psum(jnp.where(mine, value, jnp.zeros_like(value)), axis)
+    return jnp.sum(lax.all_gather(jnp.where(mine, value, jnp.zeros_like(value)), axis), axis=0)
 
 
 def shards(diag_block, panel, trailing, parent_front, front_order, dest_group, parent_block):

time: 473 us -> 524 us (1.11)
  waiting for transfers between devices: 248 us -> 294 us
    all_gather x0 -> x1, waiting for transfers between devices: none -> 51.2 us  [spread(): lax.all_gather(jnp.where(mine, value, jnp.zeros_like(value)), axis)]
    psum x1 -> x0, waiting for transfers between devices: 49.6 us -> none  [spread(): return lax.psum(jnp.where(mine, value, jnp.zeros_like(value)), axis)]
    all_gather x1, waiting for transfers between devices: 5.58 us -> 50.3 us  [shards(): lax.all_gather(panel_factor, 'col', axis=0, tiled=True)]
  transfers between devices with their start and end apart: 3 -> 3, of which waited for: 3 -> 3; matrix products, arithmetic and copies ran while one was open for 0% -> 1% of each run, Pallas kernels for 0% -> 0%
where the time goes in v1:
time: 524 us; the launch traced here: 515 us
  waiting for transfers between devices  294 us (56%)
  other arithmetic  125 us (24%)
  matrix products  38.3 us (7%)
  local copies, waits for them, and re-layouts  29.7 us (6%)
  between operations  17.4 us (3%)
  starting transfers between devices  9.78 us (2%)
    all_to_all x1, waiting for transfers between devices, shards(): lax.all_to_all(outgoing, 'cube', split_axis=0, concat_axis=0, tiled=True)  192 us
    another operation x14, other arithmetic, shards(): chol_diag = jnp.linalg.cholesky(diag_block[0])  78.6 us
    all_gather x1, waiting for transfers between devices, spread(): lax.all_gather(jnp.where(mine, value, jnp.zeros_like(value)), axis)  51.2 us
    all_gather x1, waiting for transfers between devices, shards(): lax.all_gather(panel_factor, 'col', axis=0, tiled=True)  50.3 us
    another operation x4, other arithmetic, shards(): lax.linalg.triangular_solve(chol_diag, panel[0], left_side=False, lower=T...  40.6 us
  transfers between devices with their start and end apart: 3, of which 3 were waited for; matrix products, arithmetic and copies ran while one was open for 1% of the time, Pallas kernels for 0%

profile of v1, /device:TPU:1, one launch (start us, length us, event | category | flops | bytes accessed | tf_op | source)
XLA Modules:
  0.0 514.7 jit_solution(18135571491551536149)
XLA Ops:
  6.5 1.6 copy.15
  8.1 1.4 fusion.2
  9.6 11.7 %cholesky.105 = f32[128,128]{1,0:T(8,128)S(1)} custom-call(f32[128,128]{1,0:T(8,128)S(1)} %cholesky.269), custom_call_target="Cholesky" | custom-call | tf_op jit(solution)/shard_map/jit(cholesky)/cholesky | solution.py:16
  21.3 9.8 %custom-call.30 = f32[1,128,128]{1,2,0:T(8,128)S(1)} custom-call(f32[1,128,128]{2,1,0:T(8,128)S(1)} %get-tuple-element.32), custom_call_target="InvertDiagBlocksLowerTriangular" | custom-call | tf_op jit(solution)/shard_map/jit(cholesky)/cholesky | solution.py:16
  31.9 11.7 %cholesky.219 = f32[128,128]{1,0:T(8,128)S(1)} custom-call(f32[128,128]{1,0:T(8,128)S(1)} %cholesky.273), custom_call_target="Cholesky" | custom-call | tf_op jit(solution)/shard_map/jit(cholesky)/cholesky | solution.py:16
  43.7 10.0 %custom-call.31 = f32[1,128,128]{1,2,0:T(8,128)S(1)} custom-call(f32[1,128,128]{2,1,0:T(8,128)S(1)} %get-tuple-element.29), custom_call_target="InvertDiagBlocksLowerTriangular" | custom-call | tf_op jit(solution)/shard_map/jit(cholesky)/cholesky | solution.py:16
  54.3 11.7 %cholesky.240 = f32[128,128]{1,0:T(8,128)S(1)} custom-call(f32[128,128]{1,0:T(8,128)S(1)} %cholesky.278), custom_call_target="Cholesky" | custom-call | tf_op jit(solution)/shard_map/jit(cholesky)/cholesky | solution.py:16
  66.8 9.8 %custom-call.32 = f32[1,128,128]{1,2,0:T(8,128)S(1)} custom-call(f32[1,128,128]{2,1,0:T(8,128)S(1)} %get-tuple-element.26), custom_call_target="InvertDiagBlocksLowerTriangular" | custom-call | tf_op jit(solution)/shard_map/jit(cholesky)/cholesky | solution.py:16
  77.2 11.7 %cholesky.257 = f32[128,128]{1,0:T(8,128)S(1)} custom-call(f32[128,128]{1,0:T(8,128)S(1)} %convolution_subtract_fusion.5), custom_call_target="Cholesky" | custom-call | tf_op jit(solution)/shard_map/jit(cholesky)/cholesky | solution.py:16
  92.9 8.4 %while.1 = (s32[]{:T(128)}, f32[512,512]{1,0:T(8,128)S(1)}, s32[4,2]{0,1:T(2,128)S(1)}, f32[4,128,128]{2,1,0:T(8,128)S(1)}, s32[]{:T(128)}) while((s32[]{:T(128)}, f32[512,512]{1,0:T(8,128)S(1)}, s32[4,2]{0,1:T(2,128)S(1)}, f32[4,128,128]{2,1,0:T(8,128)S(1)}, s32[]{:T(128)}) %tuple.27), condition=%wide.while_cond, body=%wide.while_body.sunk | while | flops 2 | bytes 131181 | solution.py:17
  93.8 1.3 bitcast_dynamic-update-slice_fusion.2
  95.9 1.3 bitcast_dynamic-update-slice_fusion.2
  97.9 1.3 bitcast_dynamic-update-slice_fusion.2
  100.0 1.3 bitcast_dynamic-update-slice_fusion.2
  101.3 39.3 %custom-call.33 = f32[4,128,128]{1,2,0:T(8,128)S(1)} custom-call(f32[4,128,128]{2,1,0:T(8,128)S(1)} %get-tuple-element.12), custom_call_target="InvertDiagBlocksLowerTriangular" | custom-call | tf_op jit(solution)/shard_map/triangular_solve | solution.py:17
  140.6 1.4 fusion.11
  142.0 1.5 convolution_subtract_fusion.1
  144.0 1.9 convolution_subtract_fusion
  146.4 2.4 convolution_subtract_fusion.2
  149.3 1.3 copy.17
  150.7 1.1 pad_maximum_fusion
  152.9 51.2 %all-gather.3.cloned.1.call-done = f32[4,512,512]{2,1,0:T(8,128)} async-done(((f32[1,512,512]{2,1,0:T(8,128)}), f32[4,512,512]{2,1,0:T(8,128)}) %all-gather.3.cloned.1.call-update) | async-done | bytes 4194320 | tf_op jit(solution)/shard_map/all_gather | solution.py:11
  204.1 2.8 reduce_sum.19
  206.9 50.3 %all-gather.5.cloned.1.call-done = f32[2048,512]{0,1:T(8,128)} async-done(((f32[512,512]{0,1:T(8,128)}), f32[2048,512]{0,1:T(8,128)}) %all-gather.5.cloned.1.call-update) | async-done | bytes 4194320 | tf_op jit(solution)/shard_map/all_gather | solution.py:23
  257.2 9.6 %fusion.1 = f32[64,8,16,128]{3,1,2,0:T(8,128)S(1)} fusion(f32[1,512,2048]{2,1,0:T(8,128)} %param.9, f32[512,512]{1,0:T(8,128)S(1)} %reduce_sum.19, f32[2048,512]{0,1:T(8,128)} %all-gather.5.cloned.1.call-done, pred[2048]{0:T(1024)(128)(4,1)S(1)} %add_compare_fusion), kind=kOutput, calls=%fused_computation.5 | convolution fusion | flops 6444548096 | bytes 13633536 | tf_op jit(solution)/shard_map/dot_general | solution.py:21
  268.2 3.3 copy.19
  271.4 4.9 reshape.201
  276.4 8.7 %fusion.33 = f32[16,8,16384]{2,1,0:T(8,128)} fusion(f32[64,16384,1]{1,0,2:T(8,128)} %reshape.201, s32[16,8]{1,0:T(8,128)S(1)} %multiply_add_fusion, s32[64]{0:T(128)S(1)} %multiply_add_fusion.1), kind=kOutput, calls=%fused_computation.67 | convolution fusion | flops 1610620928 | bytes 12583680 | tf_op jit(solution)/shard_map/dot_general | solution.py:59
  285.1 9.7 %all-to-all-start = ((f32[16,8,16384]{2,1,0:T(8,128)}), f32[16,8,16384]{2,1,0:T(8,128)}, u32[]{:S(2)}, u32[]{:S(2)}) async-start(f32[16,8,16384]{2,1,0:T(8,128)} %fusion.33), calls=%async_computation | async-start | bytes 16777216 | tf_op jit(solution)/shard_map/all_to_all | solution.py:60
  295.3 192.4 %all-to-all-done = f32[16,8,16384]{2,1,0:T(8,128)} async-done(((f32[16,8,16384]{2,1,0:T(8,128)}), f32[16,8,16384]{2,1,0:T(8,128)}, u32[]{:S(2)}, u32[]{:S(2)}) %all-to-all-start) | async-done | bytes 8388640 | tf_op jit(solution)/shard_map/all_to_all | solution.py:60
  487.7 9.0 %copy.20 = f32[16384,128]{1,0:T(8,128)} copy(f32[16384,128]{0,1:T(8,128)} %bitcast.30) | data formatting | bytes 16777216 | tf_op jit(solution)/shard_map/dot_general | solution.py:71
  496.7 9.4 %convolution_bitcast_fusion = f32[1,128,16,128]{3,2,1,0:T(8,128)S(1)} fusion(f32[16,128,1]{0,1,2:T(8,128)S(1)} %convolution_bitcast_fusion.1, f32[128,128,128]{2,1,0:T(8,128)} %bitcast.108), kind=kOutput, calls=%fused_computation.6 | convolution fusion | flops 402653184 | bytes 9445376 | tf_op jit(solution)/shard_map/dot_general | solution.py:71
  (58 shorter events, 11.8 us)
Async XLA Ops:
  6.5 197.6 %all-gather.3.cloned.1.call-start = ((), (), s32[]{:S(2)}) async-start(), calls=%async_computation.1 | async-start | bytes 5242880 | tf_op jit(solution)/shard_map/all_gather | solution.py:11
  149.2 3.3 copy-start.1
  150.6 106.6 %all-gather.5.cloned.1.call-start = ((), (), s32[]{:S(2)}) async-start(), calls=%async_computation.2 | async-start | bytes 5242880 | tf_op jit(solution)/shard_map/all_gather | solution.py:23
  285.1 10.0 %copy-start.2 = (s32[16,1,1,64,1]{3,4,2,1,0:T(1,128)S(1)}, s32[16,1,1,64,1]{3,4,2,1,0:T(1,128)}, u32[]{:S(2)}) copy-start(s32[16,1,1,64,1]{3,4,2,1,0:T(1,128)} %param.13) | copy-start | bytes 12292
  285.1 202.6 %all-to-all-start = ((f32[16,8,16384]{2,1,0:T(8,128)}), f32[16,8,16384]{2,1,0:T(8,128)}, u32[]{:S(2)}, u32[]{:S(2)}) async-start(f32[16,8,16384]{2,1,0:T(8,128)} %fusion.33), calls=%async_computation | async-start | bytes 16777216 | tf_op jit(solution)/shard_map/all_to_all | solution.py:60
  496.7 9.6 %copy-start = (f32[1,128,2048]{2,1,0:T(8,128)S(1)}, f32[1,128,2048]{2,1,0:T(8,128)}, u32[]{:S(2)}) copy-start(f32[1,128,2048]{2,1,0:T(8,128)} %param.10) | copy-start | bytes 3145732
Sparse Core Ops, SparseCore 0:
  150.8 53.3 all-gather.2
  205.9 51.2 all-gather.4
